TPU v7x, 32 devices: a whole 2x2x4 slice. The times are simulated.
32 devices in a mesh: dp: 2 (over core), ep: 16 (over z, y, x).
Axes of the slice: x: 2, y: 2, z: 4, core: 2. Of those that a mesh axis runs over, the one named last changes fastest.
Arguments:
- latent_cache: bfloat16 [16, 4, 512, 576], P('ep', 'dp'), may hold values from -6 to 6
- lengths: int32 [16, 4], P(None, 'dp'), may hold values from 2 to 512
- new_home: int32 [16, 4], P(None, 'dp'), may hold values from 0 to 15, as said below
- queries: bfloat16 [2, 16, 4, 128, 576], P(None, 'ep', 'dp'), may hold values from -32 to 32
- new_latent: bfloat16 [2, 16, 4, 576], P(None, 'ep', 'dp'), may hold values from -6 to 6
- hidden: bfloat16 [2, 16, 4, 3584], P(None, 'ep', 'dp'), may hold values from -6 to 6
- routes: int32 [2, 16, 4, 8], P(None, 'ep', 'dp'), may hold values from 0 to 15, all different within a row; in each aligned block of 4 rows (0 to 3, 4 to 7, ..., all dimensions but the last counted through in order) at most 4 rows name the same one
- route_logits: bfloat16 [2, 16, 4, 8], P(None, 'ep', 'dp'), may hold values from -8 to 8
- w_gate: bfloat16 [16, 3584, 1024], P('ep', None, 'dp'), may hold values from -0.09375 to 0.09375
- w_up: bfloat16 [16, 3584, 1024], P('ep', None, 'dp'), may hold values from -0.09375 to 0.09375
- w_down: bfloat16 [16, 1024, 3584], P('ep', 'dp'), may hold values from -0.1875 to 0.1875
Outputs:
- attended: bfloat16 [2, 16, 4, 128, 512], P(None, 'ep', 'dp')
- moe_out: bfloat16 [2, 16, 4, 3584], P(None, 'ep', 'dp')
Inputs may be any that keep to these rules, and one draw needn't show every extreme that they name: `routes`: in each step, the 4 requests of one ep index name any one expert in at most 4 of their choices, and this bound is reached. For each request index c, new_home[., c] exchanges exactly two ep indices and leaves every other one in place, so new_home[new_home[e, c], c] == e; the two indices lie 16 // 2 apart for even c and 1 apart (modulo 16) for odd c.
All inputs are finite; a program needn't handle non-finite values.
Results may differ from a plain program's by a relative error of at most 0.0057.
Values may be sent and summed in bfloat16 or wider, within the bound.
A program may use at most 128 MiB of HBM per device.

v0:
```python
import math

import jax
import jax.numpy as jnp
from jax import lax
from jax.sharding import PartitionSpec as P

KV_RANK = 512
HEAD_QK = 192


def spread(value, axis, source):
    kept = jnp.where(lax.axis_index(axis) == source, value, 0).astype(value.dtype)
    return lax.psum(kept, axis)


def attend(query_rows, cache_rows, fresh_rows, length, softmax_scale):
    step_count, head_count, lat_width = query_rows.shape
    flat_query = query_rows.reshape(step_count * head_count, lat_width)
    total_keys = cache_rows.shape[0]
    key_block = math.gcd(128, total_keys)
    block_count = (length + key_block - 1) // key_block

    def score_block(block_index, buffer):
        key_rows = lax.dynamic_slice_in_dim(cache_rows, block_index * key_block, key_block, 0)
        block_scores = (
            jnp.dot(flat_query, key_rows.T, preferred_element_type=jnp.float32) * softmax_scale
        )
        key_place = block_index * key_block + jnp.arange(key_block, dtype=jnp.int32)
        block_scores = jnp.where(key_place[None, :] < length, block_scores, -jnp.inf)
        return lax.dynamic_update_slice_in_dim(buffer, block_scores, block_index * key_block, 1)

    empty_scores = jnp.full((step_count * head_count, total_keys), -jnp.inf, jnp.float32)
    cache_scores = lax.fori_loop(0, block_count, score_block, empty_scores)
    fresh_scores = (
        jnp.dot(flat_query, fresh_rows.T, preferred_element_type=jnp.float32) * softmax_scale
    )
    row_step = jnp.arange(step_count * head_count, dtype=jnp.int32) // head_count
    fresh_step = jnp.arange(step_count, dtype=jnp.int32)
    fresh_scores = jnp.where(fresh_step[None, :] <= row_step[:, None], fresh_scores, -jnp.inf)
    row_max = jnp.maximum(jnp.max(cache_scores, 1), jnp.max(fresh_scores, 1))[:, None]
    cache_weights = jnp.exp(cache_scores - row_max)
    fresh_weights = jnp.exp(fresh_scores - row_max)
    row_total = jnp.sum(cache_weights, 1, keepdims=True) + jnp.sum(fresh_weights, 1, keepdims=True)
    cache_probs = (cache_weights / row_total).astype(jnp.bfloat16)
    fresh_probs = (fresh_weights / row_total).astype(jnp.bfloat16)

    def value_block(block_index, value_sum):
        key_rows = lax.dynamic_slice_in_dim(cache_rows, block_index * key_block, key_block, 0)
        prob_block = lax.dynamic_slice_in_dim(cache_probs, block_index * key_block, key_block, 1)
        return value_sum + jnp.dot(
            prob_block, key_rows[:, :KV_RANK], preferred_element_type=jnp.float32
        )

    start_sum = jnp.dot(fresh_probs, fresh_rows[:, :KV_RANK], preferred_element_type=jnp.float32)
    value_sum = lax.fori_loop(0, block_count, value_block, start_sum)
    return value_sum.astype(jnp.bfloat16).reshape(step_count, head_count, KV_RANK)


def shards(
    latent_cache,
    lengths,
    new_home,
    queries,
    new_latent,
    hidden,
    routes,
    route_logits,
    w_gate,
    w_up,
    w_down,
):
    expert_count = lax.axis_size("ep")
    own_rank = lax.axis_index("ep")
    rank_ids = jnp.arange(expert_count, dtype=jnp.int32)
    softmax_scale = HEAD_QK ** (-0.5)
    step_count = queries.shape[0]
    attended_rows = []
    for request in range(latent_cache.shape[1]):
        home_ranks = new_home[:, request]
        anchor = home_ranks[own_rank]
        first_sender = jnp.argmax(home_ranks != rank_ids)
        second_sender = home_ranks[first_sender]
        own_cache = latent_cache[0, request]
        own_query = queries[:, 0, request]
        own_fresh = new_latent[:, 0, request]
        computed = attend(
            own_query, own_cache, own_fresh, lengths[own_rank, request], softmax_scale
        )
        result = computed
        for sender in (first_sender, second_sender):
            arrived = spread(computed, "ep", sender)
            result = jnp.where((anchor == sender) & (anchor != own_rank), arrived, result)
        attended_rows.append(result)
    attended = jnp.stack(attended_rows, 1)[:, None]
    gathered = (
        lax.all_gather(hidden[:, 0], "dp", axis=1, tiled=True),
        lax.all_gather(routes[:, 0], "dp", axis=1, tiled=True),
        lax.all_gather(route_logits[:, 0], "dp", axis=1, tiled=True),
    )
    col_hidden, col_routes, col_logits = gathered
    column_rows = col_hidden.shape[1]
    top_count = routes.shape[3]
    model_width = hidden.shape[3]
    capacity = max(2, 2 * column_rows * top_count // expert_count)
    sigmoid_part = jax.nn.sigmoid(col_logits.astype(jnp.float32))
    gate_weights = 2.5 * sigmoid_part / jnp.sum(sigmoid_part, -1, keepdims=True)
    slot_ids = jnp.arange(expert_count * capacity, dtype=jnp.int32)

    def dispatch_plan(step_routes):
        flat_routes = step_routes.reshape(-1)
        onehot = (flat_routes[:, None] == rank_ids[None, :]).astype(jnp.int32)
        earlier = jnp.sum(jnp.cumsum(onehot, 0) * onehot, 1) - 1
        return flat_routes * capacity + earlier

    def build_buffer(step_hidden, placed):
        chosen = placed.reshape(column_rows, top_count)[None, :, :] == slot_ids[:, None, None]
        selector = jnp.any(chosen, 2).astype(jnp.bfloat16)
        filled = jnp.dot(selector, step_hidden, preferred_element_type=jnp.float32).astype(
            jnp.bfloat16
        )
        return filled.reshape(expert_count, capacity, model_width)

    def expert_math(received):
        source_count, item_count, _ = received.shape
        flat_rows = received.reshape(source_count * item_count, model_width)
        gate_part = jnp.dot(flat_rows, w_gate[0], preferred_element_type=jnp.float32)
        up_part = jnp.dot(flat_rows, w_up[0], preferred_element_type=jnp.float32)
        hidden_units = (jax.nn.silu(gate_part) * up_part).astype(jnp.bfloat16)
        partial_value = jnp.dot(hidden_units, w_down[0], preferred_element_type=jnp.float32).astype(
            jnp.bfloat16
        )
        return partial_value.reshape(source_count, item_count, model_width)

    def expert_apart(received):
        return lax.all_to_all(expert_math(received), "ep", split_axis=0, concat_axis=0, tiled=True)

    def combine(returned, placed, step_gates):
        flat_out = returned.reshape(expert_count * capacity, model_width)
        picked = jnp.take(flat_out, placed, axis=0).astype(jnp.float32)
        weighted = picked * step_gates.reshape(-1)[:, None]
        return jnp.sum(weighted.reshape(column_rows, top_count, model_width), 1)

    placements = [dispatch_plan(col_routes[number]) for number in range(step_count)]
    buffers = [build_buffer(col_hidden[number], placements[number]) for number in range(step_count)]
    returned_list = [
        expert_apart(lax.all_to_all(buffers[number], "ep", split_axis=0, concat_axis=0, tiled=True))
        for number in range(step_count)
    ]
    partials = jnp.stack(
        [
            combine(returned_list[number], placements[number], gate_weights[number])
            for number in range(step_count)
        ],
        0,
    )
    summed = lax.psum_scatter(partials, "dp", scatter_dimension=1, tiled=True)
    moe_out = summed.astype(jnp.bfloat16)[:, None]
    return (attended, moe_out)


def solution(mesh):
    placed = (
        P("ep", "dp", None, None),
        P(None, "dp"),
        P(None, "dp"),
        P(None, "ep", "dp", None, None),
        P(None, "ep", "dp", None),
        P(None, "ep", "dp", None),
        P(None, "ep", "dp", None),
        P(None, "ep", "dp", None),
        P("ep", None, "dp"),
        P("ep", None, "dp"),
        P("ep", "dp", None),
    )
    return jax.shard_map(
        shards,
        mesh=mesh,
        in_specs=placed,
        out_specs=(P(None, "ep", "dp", None, None), P(None, "ep", "dp", None)),
        check_vma=False,
    )
```

profile of v0, /device:TPU:0, one launch (start us, length us, event | category | flops | bytes accessed | tf_op | source)
XLA Modules:
  0.0 191.5 jit_solution(3648106268967699894)
XLA Ops:
  7.9 2.0 %all-gather = s32[2,1,4,8]{3,0,1,2:T(2,128)S(1)} all-gather(s32[2,1,2,8]{3,0,1,2:T(2,128)S(1)} %copy.84), channel_id=2, replica_groups=mesh['dp'=2,'ep'=16] {'dp'}, dimensions={2}, use_global_device_ids=true | all-gather | bytes 384 | tf_op jit(solution)/shard_map/all_gather | solution.py:98
  10.5 0.8 copy.85
  11.3 1.8 all-gather.1
  13.6 0.9 reshape.131
  14.5 8.2 %all-to-all-start = ((bf16[16,4,3584]{2,1,0:T(4,128)(2,1)}), bf16[16,4,3584]{2,1,0:T(4,128)(2,1)}, u32[]{:S(2)}, u32[]{:S(2)}) async-start(bf16[16,4,3584]{2,1,0:T(4,128)(2,1)} %reshape.131), calls=%async_computation | async-start | bytes 917504 | tf_op jit(solution)/shard_map/all_to_all | solution.py:147
  22.8 1.4 compare_reduce_fusion
  25.4 0.8 fusion.85
  26.8 1.4 constant_dynamic-slice_fusion.1
  28.9 1.3 fusion.80
  30.5 0.8 fusion.81
  31.6 0.9 while.40
  37.2 1.2 copy.80
  38.4 1.0 while.42
  45.7 0.8 broadcast_select_fusion.2
  46.5 0.8 broadcast_select_fusion
  47.4 1.8 all-gather.2
  50.2 0.9 reshape.136
  51.2 12.1 %all-to-all-start.2 = ((bf16[16,4,3584]{2,1,0:T(4,128)(2,1)}), bf16[16,4,3584]{2,1,0:T(4,128)(2,1)S(1)}, u32[]{:S(2)}, u32[]{:S(2)}) async-start(bf16[16,4,3584]{2,1,0:T(4,128)(2,1)} %reshape.136), calls=%async_computation.2 | async-start | bytes 917504 | tf_op jit(solution)/shard_map/all_to_all | solution.py:147
  63.3 1.1 reshape.132
  64.4 2.8 %fusion.24 = f32[64,512]{1,0:T(8,128)S(1)} fusion(bf16[64,3584]{1,0:T(8,128)(2,1)S(1)} %reshape.132, bf16[1,3584,512]{2,1,0:T(8,128)(2,1)} %param.29), kind=kOutput, calls=%fused_computation.36 | convolution fusion | flops 234881024 | bytes 4259840 | tf_op jit(solution)/shard_map/dot_general | solution.py:127
  67.2 4.6 %convolution_convert_fusion.1 = bf16[64,3584]{1,0:T(8,128)(2,1)S(1)} fusion(bf16[1,512,3584]{2,1,0:T(8,128)(2,1)} %param.31, bf16[64,3584]{1,0:T(8,128)(2,1)S(1)} %reshape.132, bf16[1,3584,512]{2,1,0:T(8,128)(2,1)} %param.30, f32[64,512]{1,0:T(8,128)S(1)} %fusion.24), kind=kOutput, calls=%fused_computation.25 | convolution fusion | flops 470188032 | bytes 8388608 | tf_op jit(solution)/shard_map/dot_general | solution.py:130
  71.8 0.9 reshape.133
  72.7 9.0 %all-to-all-done.2 = bf16[16,4,3584]{2,1,0:T(4,128)(2,1)S(1)} async-done(((bf16[16,4,3584]{2,1,0:T(4,128)(2,1)}), bf16[16,4,3584]{2,1,0:T(4,128)(2,1)S(1)}, u32[]{:S(2)}, u32[]{:S(2)}) %all-to-all-start.2) | async-done | bytes 458784 | tf_op jit(solution)/shard_map/all_to_all | solution.py:147
  81.8 4.7 %all-to-all-start.1 = ((bf16[16,4,3584]{2,1,0:T(4,128)(2,1)}), bf16[16,4,3584]{2,1,0:T(4,128)(2,1)S(1)}, u32[]{:S(2)}, u32[]{:S(2)}) async-start(bf16[16,4,3584]{2,1,0:T(4,128)(2,1)} %reshape.133), calls=%async_computation.1 | async-start | bytes 917504 | tf_op jit(solution)/shard_map/all_to_all | solution.py:136
  86.6 2.8 %fusion.22 = f32[64,512]{1,0:T(8,128)S(1)} fusion(bf16[64,3584]{1,0:T(8,128)(2,1)S(1)} %reshape.137, bf16[1,3584,512]{2,1,0:T(8,128)(2,1)} %param.29), kind=kOutput, calls=%fused_computation.34 | convolution fusion | flops 234881024 | bytes 4259840 | tf_op jit(solution)/shard_map/dot_general | solution.py:127
  89.4 4.6 %convolution_convert_fusion = bf16[64,3584]{1,0:T(8,128)(2,1)S(1)} fusion(bf16[1,512,3584]{2,1,0:T(8,128)(2,1)} %param.31, bf16[64,3584]{1,0:T(8,128)(2,1)S(1)} %reshape.137, bf16[1,3584,512]{2,1,0:T(8,128)(2,1)} %param.30, f32[64,512]{1,0:T(8,128)S(1)} %fusion.22), kind=kOutput, calls=%fused_computation.24 | convolution fusion | flops 470188032 | bytes 8388608 | tf_op jit(solution)/shard_map/dot_general | solution.py:130
  94.1 0.9 reshape.138
  95.0 6.5 %all-to-all-done.1 = bf16[16,4,3584]{2,1,0:T(4,128)(2,1)S(1)} async-done(((bf16[16,4,3584]{2,1,0:T(4,128)(2,1)}), bf16[16,4,3584]{2,1,0:T(4,128)(2,1)S(1)}, u32[]{:S(2)}, u32[]{:S(2)}) %all-to-all-start.1) | async-done | bytes 458784 | tf_op jit(solution)/shard_map/all_to_all | solution.py:136
  101.5 3.6 %all-to-all-start.3 = ((bf16[16,4,3584]{2,1,0:T(4,128)(2,1)}), bf16[16,4,3584]{2,1,0:T(4,128)(2,1)S(1)}, u32[]{:S(2)}, u32[]{:S(2)}) async-start(bf16[16,4,3584]{2,1,0:T(4,128)(2,1)} %reshape.138), calls=%async_computation.3 | async-start | bytes 917504 | tf_op jit(solution)/shard_map/all_to_all | solution.py:136
  112.9 64.2 %all-reduce.4.cloned.1.call-done = (bf16[2,128,512]{2,1,0:T(8,128)(2,1)}, bf16[2,128,512]{2,1,0:T(8,128)(2,1)}, bf16[2,128,512]{2,1,0:T(8,128)(2,1)}, bf16[2,128,512]{2,1,0:T(8,128)(2,1)}) async-done(((bf16[2,128,512]{2,1,0:T(8,128)(2,1)}, bf16[2,128,512]{2,1,0:T(8,128)(2,1)}, bf16[2,128,512]{2,1,0:T(8,128)(2,1)}, bf16[2,128,512]{2,1,0:T(8,128)(2,1)}), (bf16[2,128,512]{2,1,0:T(8,128)(2,1)}, ...) | async-done | bytes 1048592 | tf_op jit(solution)/shard_map/psum | solution.py:14
  177.3 0.8 maximum_bitcast_fusion
  180.2 3.8 %all-reduce = bf16[2,4,3584]{2,1,0:T(4,128)(2,1)S(1)} all-reduce(f32[2,4,3584]{2,1,0:T(4,128)S(1)} %pad_maximum_fusion), channel_id=5, replica_groups=mesh['dp'=2,'ep'=16] {'dp'}, use_global_device_ids=true, to_apply=%region_31.33.clone | all-reduce | flops 28672 | bytes 172032
  (99 shorter events, 15.5 us)
Async XLA Ops:
  7.2 23.3 %copy-start = (bf16[2,1,2,128,576]{3,4,2,1,0:T(8,128)(2,1)S(1)}, bf16[2,1,2,128,576]{3,4,2,1,0:T(8,128)(2,1)}, u32[]{:S(2)}) copy-start(bf16[2,1,2,128,576]{3,4,2,1,0:T(8,128)(2,1)} %param.24) | copy-start | bytes 1769476
  10.3 1.0 copy-start.2
  14.5 36.7 %all-to-all-start = ((bf16[16,4,3584]{2,1,0:T(4,128)(2,1)}), bf16[16,4,3584]{2,1,0:T(4,128)(2,1)}, u32[]{:S(2)}, u32[]{:S(2)}) async-start(bf16[16,4,3584]{2,1,0:T(4,128)(2,1)} %reshape.131), calls=%async_computation | async-start | bytes 917504 | tf_op jit(solution)/shard_map/all_to_all | solution.py:147
  22.7 154.4 %all-reduce.4.cloned.1.call-start = ((), (), s32[]{:S(2)}) async-start(), calls=%async_computation.4 | async-start | bytes 2097152 | tf_op jit(solution)/shard_map/psum | solution.py:14
  30.5 2.3 %copy-start.1 = (bf16[2,1,2,576]{3,2,1,0:T(2,128)(2,1)S(1)}, bf16[2,1,2,576]{3,2,1,0:T(2,128)(2,1)}, u32[]{:S(2)}) copy-start(bf16[2,1,2,576]{3,2,1,0:T(2,128)(2,1)} %param.25) | copy-start | bytes 13828
  31.6 2.3 %copy-start.4 = (s32[16,2]{0,1:T(2,128)S(1)}, s32[16,2]{0,1:T(2,128)}, u32[]{:S(2)}) copy-start(s32[16,2]{0,1:T(2,128)} %param.23) | copy-start | bytes 388
  42.9 2.8 %copy-start.5 = (bf16[2,1,2,8]{3,2,1,0:T(2,128)(2,1)S(1)}, bf16[2,1,2,8]{3,2,1,0:T(2,128)(2,1)}, u32[]{:S(2)}) copy-start(bf16[2,1,2,8]{3,2,1,0:T(2,128)(2,1)} %param.28) | copy-start | bytes 196
  51.2 30.5 %all-to-all-start.2 = ((bf16[16,4,3584]{2,1,0:T(4,128)(2,1)}), bf16[16,4,3584]{2,1,0:T(4,128)(2,1)S(1)}, u32[]{:S(2)}, u32[]{:S(2)}) async-start(bf16[16,4,3584]{2,1,0:T(4,128)(2,1)} %reshape.136), calls=%async_computation.2 | async-start | bytes 917504 | tf_op jit(solution)/shard_map/all_to_all | solution.py:147
  67.2 19.3 %copy-start.3 = (s32[32]{0:T(128)S(1)}, s32[32]{0:T(128)}, u32[]{:S(2)}) copy-start(s32[32]{0:T(128)} %copy-done.2) | copy-start | bytes 388
  81.8 19.7 %all-to-all-start.1 = ((bf16[16,4,3584]{2,1,0:T(4,128)(2,1)}), bf16[16,4,3584]{2,1,0:T(4,128)(2,1)S(1)}, u32[]{:S(2)}, u32[]{:S(2)}) async-start(bf16[16,4,3584]{2,1,0:T(4,128)(2,1)} %reshape.133), calls=%async_computation.1 | async-start | bytes 917504 | tf_op jit(solution)/shard_map/all_to_all | solution.py:136
  89.4 22.3 %copy-start.6 = (u32[32]{0:T(128)S(1)}, u32[32]{0:T(128)}, u32[]{:S(2)}) copy-start(u32[32]{0:T(128)} %constant.148) | copy-start | bytes 388
  101.5 77.4 %all-to-all-start.3 = ((bf16[16,4,3584]{2,1,0:T(4,128)(2,1)}), bf16[16,4,3584]{2,1,0:T(4,128)(2,1)S(1)}, u32[]{:S(2)}, u32[]{:S(2)}) async-start(bf16[16,4,3584]{2,1,0:T(4,128)(2,1)} %reshape.138), calls=%async_computation.3 | async-start | bytes 917504 | tf_op jit(solution)/shard_map/all_to_all | solution.py:136
Sparse Core Ops, SparseCore 0:
  47.5 129.5 all-reduce.3
where the time goes:
time: 193 us; the launch traced here: 191 us
  waiting for transfers between devices  79.8 us (41%)
  between operations  29 us (15%)
  starting transfers between devices  28.7 us (15%)
  matrix products  17.5 us (9%)
  local copies, waits for them, and re-layouts  17.1 us (9%)
  other arithmetic  9.87 us (5%)
  blocking collectives  9.41 us (5%)
    psum x1, waiting for transfers between devices, spread(): return lax.psum(kept, axis)  64.2 us
    all_to_all x2, starting transfers between devices, shards(): lax.all_to_all(buffers[number], 'ep', split_axis=0, concat_axis=0, tiled=...  20.3 us
    dot_general x2, matrix products, expert_math(): jnp.dot(hidden_units, w_down[0], preferred_element_type=jnp.float32)  9.26 us
    all_to_all x2, waiting for transfers between devices, shards(): lax.all_to_all(buffers[number], 'ep', split_axis=0, concat_axis=0, tiled=...  9.01 us
    all_to_all x2, starting transfers between devices, expert_apart(): lax.all_to_all(expert_math(received), 'ep', split_axis=0, concat_axis=0,...  8.38 us
    all_to_all x2, waiting for transfers between devices, expert_apart(): lax.all_to_all(expert_math(received), 'ep', split_axis=0, concat_axis=0,...  6.52 us
    dot_general x2, matrix products, expert_math(): jnp.dot(flat_rows, w_gate[0], preferred_element_type=jnp.float32)  5.57 us
  transfers between devices with their start and end apart: 5, of which 3 were waited for; matrix products, arithmetic and copies ran while one was open for 20% of the time, Pallas kernels for 0%

commit v1 on v0

v1 whole, which is shorter than its diff:
```python
import jax
import jax.numpy as jnp
from jax import lax
from jax.experimental import pallas as pl
from jax.experimental.pallas import tpu as pltpu
from jax.sharding import PartitionSpec as P

KV_RANK = 512
HEAD_QK = 192


def attend_kernel(length_ref, query_ref, cache_ref, fresh_ref, out_ref):
    step_count, head_count, lat_width = query_ref.shape
    rows = step_count * head_count
    length = length_ref[pl.program_id(0)]
    scale = HEAD_QK ** (-0.5)
    query = query_ref[...].reshape(rows, lat_width)
    keys = cache_ref[...]
    scores = (
        lax.dot_general(
            query, keys, (((1,), (1,)), ((), ())), preferred_element_type=jnp.float32
        )
        * scale
    )
    place = lax.broadcasted_iota(jnp.int32, scores.shape, 1)
    scores = jnp.where(place < length, scores, -jnp.inf)
    row_step = lax.broadcasted_iota(jnp.int32, (rows, 1), 0) // head_count
    wide_query = query.astype(jnp.float32)
    fresh = fresh_ref[...].astype(jnp.float32)
    fresh_scores = []
    row_max = jnp.max(scores, 1, keepdims=True)
    for step in range(step_count):
        one = jnp.sum(wide_query * fresh[step : step + 1], 1, keepdims=True) * scale
        one = jnp.where(row_step >= step, one, -jnp.inf)
        row_max = jnp.maximum(row_max, one)
        fresh_scores.append(one)
    weights = jnp.exp(scores - row_max)
    fresh_weights = [jnp.exp(one - row_max) for one in fresh_scores]
    total = jnp.sum(weights, 1, keepdims=True)
    for one in fresh_weights:
        total = total + one
    probs = (weights / total).astype(jnp.bfloat16)
    served = jnp.dot(probs, keys[:, :KV_RANK], preferred_element_type=jnp.float32)
    for step in range(step_count):
        part = (fresh_weights[step] / total).astype(jnp.bfloat16).astype(jnp.float32)
        served = served + part * fresh[step : step + 1, :KV_RANK]
    out_ref[...] = served.astype(jnp.bfloat16).reshape(step_count, head_count, KV_RANK)


def attend(own_lengths, queries, cache, fresh):
    step_count, _, requests, heads, lat = queries.shape
    keys = cache.shape[2]
    return pl.pallas_call(
        attend_kernel,
        grid_spec=pltpu.PrefetchScalarGridSpec(
            num_scalar_prefetch=1,
            grid=(requests,),
            in_specs=[
                pl.BlockSpec((step_count, None, None, heads, lat), lambda r, n: (0, 0, r, 0, 0)),
                pl.BlockSpec((None, None, keys, lat), lambda r, n: (0, r, 0, 0)),
                pl.BlockSpec((None, step_count, lat), lambda r, n: (r, 0, 0)),
            ],
            out_specs=pl.BlockSpec((None, step_count, heads, KV_RANK), lambda r, n: (r, 0, 0, 0)),
        ),
        out_shape=jax.ShapeDtypeStruct((requests, step_count, heads, KV_RANK), jnp.bfloat16),
        name="attend",
    )(own_lengths, queries, cache, fresh)


def relocate(computed, new_home, ranks, own_rank):
    requests = computed.shape[0]
    half = ranks // 2
    across = [(e, (e + half) % ranks) for e in range(ranks)]
    ahead = [(e, (e + 1) % ranks) for e in range(ranks)]
    behind = [(e, (e - 1) % ranks) for e in range(ranks)]
    even, odd = computed[0::2], computed[1::2]
    far = lax.ppermute(even, "ep", across)
    left = lax.ppermute(odd, "ep", ahead)
    right = lax.ppermute(odd, "ep", behind)
    anchor = new_home[own_rank]
    results = []
    for request in range(requests):
        home, slot = anchor[request], request // 2
        if request % 2 == 0:
            moved = far[slot]
        else:
            moved = jnp.where(home == (own_rank + 1) % ranks, right[slot], left[slot])
        results.append(jnp.where(home == own_rank, computed[request], moved))
    return jnp.stack(results, 1)[:, None]


def shards(
    latent_cache,
    lengths,
    new_home,
    queries,
    new_latent,
    hidden,
    routes,
    route_logits,
    w_gate,
    w_up,
    w_down,
):
    ranks = lax.axis_size("ep")
    own_rank = lax.axis_index("ep")
    step_count, _, requests, width = hidden.shape
    own_rows = step_count * requests
    slices = lax.axis_size("dp")

    def shift(value, step):
        return lax.ppermute(value, "dp", [(i, (i + step) % slices) for i in range(slices)])

    rows = hidden.reshape(own_rows, width)
    copies = jnp.broadcast_to(rows[None], (ranks, own_rows, width))
    mine = lax.all_to_all(copies, "ep", split_axis=0, concat_axis=0, tiled=True)
    mine = mine.reshape(ranks * own_rows, width)

    computed = attend(
        lengths[own_rank], queries, latent_cache, jnp.swapaxes(new_latent[:, 0], 0, 1)
    )
    attended = relocate(computed, new_home, ranks, own_rank)

    tokens = jnp.concatenate([mine] + [shift(mine, step) for step in range(1, slices)], 0)
    gate_part = jnp.dot(tokens, w_gate[0], preferred_element_type=jnp.float32)
    up_part = jnp.dot(tokens, w_up[0], preferred_element_type=jnp.float32)
    units = (jax.nn.silu(gate_part) * up_part).astype(jnp.bfloat16)
    slice_out = jnp.dot(units, w_down[0], preferred_element_type=jnp.float32).astype(jnp.bfloat16)
    parts = slice_out.reshape(slices, ranks * own_rows, width)
    whole = parts[0].astype(jnp.float32)
    for step in range(1, slices):
        whole = whole + shift(parts[step], -step).astype(jnp.float32)
    whole = whole.astype(jnp.bfloat16)
    returned = lax.all_to_all(
        whole.reshape(ranks, own_rows, width), "ep", split_axis=0, concat_axis=0, tiled=True
    )

    sigmoid_part = jax.nn.sigmoid(route_logits[:, 0].astype(jnp.float32))
    gates = 2.5 * sigmoid_part / jnp.sum(sigmoid_part, -1, keepdims=True)
    rank_ids = jnp.arange(ranks, dtype=jnp.int32)
    chosen = routes[:, 0, :, :, None] == rank_ids
    dense = jnp.sum(jnp.where(chosen, gates[..., None], 0.0), 2).reshape(own_rows, ranks)
    summed = jnp.sum(returned.astype(jnp.float32) * dense.T[:, :, None], 0)
    moe_out = summed.astype(jnp.bfloat16).reshape(step_count, 1, requests, width)
    return (attended, moe_out)


def solution(mesh):
    placed = (
        P("ep", "dp", None, None),
        P(None, "dp"),
        P(None, "dp"),
        P(None, "ep", "dp", None, None),
        P(None, "ep", "dp", None),
        P(None, "ep", "dp", None),
        P(None, "ep", "dp", None),
        P(None, "ep", "dp", None),
        P("ep", None, "dp"),
        P("ep", None, "dp"),
        P("ep", "dp", None),
    )
    return jax.shard_map(
        shards,
        mesh=mesh,
        in_specs=placed,
        out_specs=(P(None, "ep", "dp", None, None), P(None, "ep", "dp", None)),
        check_vma=False,
    )
```

time: 193 us -> 74.8 us (0.39)
  waiting for transfers between devices: 79.8 us -> 29.9 us
  between operations: 29 us -> 2.72 us
  matrix products: 17.5 us -> 7.15 us
  starting transfers between devices: 28.7 us -> 18.6 us
  blocking collectives: 9.41 us -> 0 us
  other arithmetic: 9.87 us -> 0.81 us
  local copies, waits for them, and re-layouts: 17.1 us -> 10.9 us
  Pallas kernels: 0 us -> 4.27 us
    psum x1 -> x0, waiting for transfers between devices: 64.2 us -> none  [spread(): return lax.psum(kept, axis)]
    ppermute x0 -> x5, waiting for transfers between devices: none -> 14.5 us  [the longest x1 11.3 us: relocate(): far = lax.ppermute(even, 'ep', across)]
    all_to_all x4 -> x2, starting transfers between devices: 28.7 us -> 15.3 us  [the longest x1 8.34 us: shards(): mine = lax.all_to_all(copies, 'ep', split_axis=0, concat_axis=0, tiled=True)]
    dot_general x14 -> x2, matrix products: 17.5 us -> 7.15 us  [the longest x1 4.46 us: shards(): jnp.dot(units, w_down[0], preferred_element_type=jnp.float32)]
    all_gather x3 -> x0, blocking collectives: 5.63 us -> none  [the longest x1 1.97 us: shards(): lax.all_gather(routes[:, 0], 'dp', axis=1, tiled=True)]
    pallas_call x0 -> x1, Pallas kernels: none -> 4.27 us  [attend(): pl.pallas_call(attend_kernel, grid_spec=pltpu.PrefetchScalarGridSpec(num_...]
    reshape x8 -> x2, local copies, waits for them, and re-layouts: 4.99 us -> 0.98 us  [the longest x1 0.87 us: shards(): whole.reshape(ranks, own_rows, width)]
    unnamed x1 -> x0, blocking collectives: 3.78 us -> none
  transfers between devices with their start and end apart: 5 -> 7, of which waited for: 3 -> 5; matrix products, arithmetic and copies ran while one was open for 20% -> 12% of each run, Pallas kernels for 0% -> 6%
where the time goes in v1:
time: 74.8 us; the launch traced here: 74.3 us
  waiting for transfers between devices  29.9 us (40%)
  starting transfers between devices  18.6 us (25%)
  local copies, waits for them, and re-layouts  10.9 us (15%)
  matrix products  7.15 us (10%)
  Pallas kernels  4.27 us (6%)
  between operations  2.72 us (4%)
  other arithmetic  0.81 us (1%)
    ppermute x1, waiting for transfers between devices, relocate(): far = lax.ppermute(even, 'ep', across)  11.3 us
    all_to_all x1, waiting for transfers between devices, shards(): mine = lax.all_to_all(copies, 'ep', split_axis=0, concat_axis=0, tiled=True)  9.73 us
    all_to_all x1, starting transfers between devices, shards(): mine = lax.all_to_all(copies, 'ep', split_axis=0, concat_axis=0, tiled=True)  8.34 us
    all_to_all x1, starting transfers between devices, shards(): lax.all_to_all(whole.reshape(ranks, own_rows, width), 'ep', split_axis=0,...  6.99 us
    all_to_all x1, waiting for transfers between devices, shards(): lax.all_to_all(whole.reshape(ranks, own_rows, width), 'ep', split_axis=0,...  5.7 us
    unnamed x19, local copies, waits for them, and re-layouts  5.01 us
    dot_general x1, matrix products, shards(): jnp.dot(units, w_down[0], preferred_element_type=jnp.float32)  4.46 us
    pallas_call x1, Pallas kernels, attend(): pl.pallas_call(attend_kernel, grid_spec=pltpu.PrefetchScalarGridSpec(num_...  4.27 us
  transfers between devices with their start and end apart: 7, of which 5 were waited for; matrix products, arithmetic and copies ran while one was open for 12% of the time, Pallas kernels for 6%

profile of v1, /device:TPU:0, one launch (start us, length us, event | category | flops | bytes accessed | tf_op | source)
XLA Modules:
  0.0 74.3 jit_solution(15714105724396921922)
XLA Ops:
  0.7 0.8 %broadcast_in_dim.27 = bf16[4,3584]{1,0:T(4,128)(2,1)S(1)} reshape(bf16[2,1,2,3584]{3,2,1,0:T(2,128)(2,1)} %param.16) | data formatting | bytes 57344 | tf_op jit(solution)/shard_map/broadcast_in_dim | solution.py:115
  1.5 0.9 %broadcast_in_dim.28 = bf16[16,4,3584]{2,1,0:T(4,128)(2,1)} broadcast(bf16[4,3584]{1,0:T(4,128)(2,1)S(1)} %broadcast_in_dim.27), dimensions={1,2} | broadcast | bytes 487424 | tf_op jit(solution)/shard_map/broadcast_in_dim | solution.py:115
  2.4 8.3 %all-to-all-start = ((bf16[16,4,3584]{2,1,0:T(4,128)(2,1)}), bf16[16,4,3584]{2,1,0:T(4,128)(2,1)S(1)}, u32[]{:S(2)}, u32[]{:S(2)}) async-start(bf16[16,4,3584]{2,1,0:T(4,128)(2,1)} %broadcast_in_dim.28), calls=%async_computation | async-start | bytes 917504 | tf_op jit(solution)/shard_map/all_to_all | solution.py:116
  10.7 2.4 %copy.20.cache_ref = bf16[1,2,512,576]{3,2,1,0:T(8,128)(2,1)} copy(bf16[1,2,512,576]{2,3,1,0:T(8,128)(2,1)} %param.11) | data formatting | bytes 2359296 | tf_op args[0]
  13.1 1.1 %copy.19.query_ref = bf16[2,1,2,128,576]{4,3,2,1,0:T(8,128)(2,1)} copy(bf16[2,1,2,128,576]{3,4,2,1,0:T(8,128)(2,1)S(1)} %copy-done.1) | data formatting | bytes 1179648 | tf_op args[3]
  14.2 0.6 copy.24
  14.8 9.7 %all-to-all-done = bf16[16,4,3584]{2,1,0:T(4,128)(2,1)S(1)} async-done(((bf16[16,4,3584]{2,1,0:T(4,128)(2,1)}), bf16[16,4,3584]{2,1,0:T(4,128)(2,1)S(1)}, u32[]{:S(2)}, u32[]{:S(2)}) %all-to-all-start) | async-done | bytes 458784 | tf_op jit(solution)/shard_map/all_to_all | solution.py:116
  24.6 0.1 reshape.104
  24.8 1.8 %collective-permute-done.3 = bf16[64,3584]{1,0:T(8,128)(2,1)S(1)} collective-permute-done((bf16[64,3584]{1,0:T(8,128)(2,1)S(1)}, bf16[64,3584]{1,0:T(8,128)(2,1)S(1)}, u32[]{:S(2)}, u32[]{:S(2)}) %collective-permute-start.3) | collective-permute-done | bytes 458784 | tf_op jit(solution)/shard_map/ppermute | solution.py:112
  26.6 2.7 %fusion.1 = f32[128,512]{1,0:T(8,128)S(1)} fusion(bf16[128,3584]{1,0:T(8,128)(2,1)S(1)} %constant_dynamic-update-slice_fusion, bf16[1,3584,512]{2,1,0:T(8,128)(2,1)} %param.20), kind=kOutput, calls=%fused_computation.2 | convolution fusion | flops 469762048 | bytes 4849664 | tf_op jit(solution)/shard_map/dot_general | solution.py:126
  29.3 4.5 %convolution_convert_fusion = bf16[128,3584]{1,0:T(8,128)(2,1)S(1)} fusion(bf16[1,512,3584]{2,1,0:T(8,128)(2,1)} %param.21, f32[128,512]{1,0:T(8,128)S(1)} %fusion.1, bf16[128,3584]{1,0:T(8,128)(2,1)S(1)} %constant_dynamic-update-slice_fusion, bf16[1,3584,512]{2,1,0:T(8,128)(2,1)} %param.19), kind=kOutput, calls=%fused_computation | convolution fusion | flops 940376064 | bytes 9437184 | tf_op jit(solution)/shard_map/dot_general | solution.py:128
  33.9 0.2 collective-permute-start.4
  34.0 0.7 dynamic-slice_reduce_fusion
  34.7 4.3 %attend.1 = bf16[2,2,128,512]{3,2,1,0:T(8,128)(2,1)} custom-call(s32[2]{0:T(128)} %get-tuple-element.14.length_ref, bf16[2,1,2,128,576]{4,3,2,1,0:T(8,128)(2,1)} %copy.19.query_ref, bf16[1,2,512,576]{3,2,1,0:T(8,128)(2,1)} %copy.20.cache_ref, bf16[2,2,576]{2,1,0:T(2,128)(2,1)} %bitcast.34), custom_call_target="tpu_custom_call" | custom-call | tf_op jit(solution)/shard_map/attend/pallas_call | solution.py:53
  39.0 1.1 %fusion.12 = (bf16[1,2,128,512]{3,2,1,0:T(8,128)(2,1)S(1)}, bf16[1,2,128,512]{3,2,1,0:T(8,128)(2,1)S(1)}) fusion(bf16[2,2,128,512]{3,2,1,0:T(8,128)(2,1)} %attend.1), kind=kLoop, calls=%fused_computation.24 | loop fusion | bytes 1048576 | tf_op jit(solution)/shard_map/slice | solution.py:88
  40.1 2.4 %collective-permute-start.1 = (bf16[1,2,128,512]{3,2,1,0:T(8,128)(2,1)S(1)}, bf16[1,2,128,512]{3,2,1,0:T(8,128)(2,1)S(1)}, u32[]{:S(2)}, u32[]{:S(2)}) collective-permute-start(bf16[1,2,128,512]{3,2,1,0:T(8,128)(2,1)S(1)} %get-tuple-element.11), channel_id=1, source_target_pairs={{0,15},{1,0},{2,1},{3,2},{4,3},{5,4},{6,5},{7,6},{8,7},{9,8},{10,9... | collective-permute-start | bytes 786440 | tf_op jit(solution)/shard_map/ppermute | solution.py:79
  42.6 0.6 collective-permute-start
  43.1 0.6 fusion.13
  45.6 0.1 add_convert_fusion
  45.8 0.9 %reshape.105 = bf16[16,4,3584]{2,1,0:T(4,128)(2,1)} reshape(bf16[64,3584]{1,0:T(8,128)(2,1)S(1)} %add_convert_fusion) | data formatting | bytes 917504 | tf_op jit(solution)/shard_map/reshape | solution.py:135
  46.6 7.0 %all-to-all-start.1 = ((bf16[16,4,3584]{2,1,0:T(4,128)(2,1)}), bf16[16,4,3584]{2,1,0:T(4,128)(2,1)S(1)}, u32[]{:S(2)}, u32[]{:S(2)}) async-start(bf16[16,4,3584]{2,1,0:T(4,128)(2,1)} %reshape.105), calls=%async_computation.1 | async-start | bytes 917504 | tf_op jit(solution)/shard_map/all_to_all | solution.py:134
  53.6 0.1 fusion.11
  53.7 0.1 bitcast_divide_fusion
  53.8 0.1 select_reduce_fusion
  53.9 0.1 copy.21
  54.0 1.4 %collective-permute-done.2 = bf16[1,2,128,512]{3,2,1,0:T(8,128)(2,1)S(1)} collective-permute-done((bf16[1,2,128,512]{3,2,1,0:T(8,128)(2,1)S(1)}, bf16[1,2,128,512]{3,2,1,0:T(8,128)(2,1)S(1)}, u32[]{:S(2)}, u32[]{:S(2)}) %collective-permute-start.2) | collective-permute-done | bytes 262176 | tf_op jit(solution)/shard_map/ppermute | solution.py:78
  55.4 11.3 %collective-permute-done = bf16[1,2,128,512]{3,2,1,0:T(8,128)(2,1)} collective-permute-done((bf16[1,2,128,512]{3,2,1,0:T(8,128)(2,1)S(1)}, bf16[1,2,128,512]{3,2,1,0:T(8,128)(2,1)}, u32[]{:S(2)}, u32[]{:S(2)}) %collective-permute-start) | collective-permute-done | bytes 262176 | tf_op jit(solution)/shard_map/ppermute | solution.py:77
  66.7 0.1 select_bitcast_fusion.1
  66.9 0.8 %copy.22 = bf16[2,1,2,128,512]{4,3,2,1,0:T(8,128)(2,1)} copy(bf16[2,1,2,128,512]{4,3,0,2,1:T(8,128)(2,1)S(1)} %maximum_bitcast_fusion) | data formatting | bytes 1048576
  67.7 5.7 %all-to-all-done.1 = bf16[16,4,3584]{2,1,0:T(4,128)(2,1)S(1)} async-done(((bf16[16,4,3584]{2,1,0:T(4,128)(2,1)}), bf16[16,4,3584]{2,1,0:T(4,128)(2,1)S(1)}, u32[]{:S(2)}, u32[]{:S(2)}) %all-to-all-start.1) | async-done | bytes 458784 | tf_op jit(solution)/shard_map/all_to_all | solution.py:134
  73.4 0.3 multiply_reduce_fusion
  73.7 0.6 convert_element_type.47
  (22 shorter events, 0.3 us)
Async XLA Ops:
  0.6 12.5 %copy-start.1 = (bf16[2,1,2,128,576]{3,4,2,1,0:T(8,128)(2,1)S(1)}, bf16[2,1,2,128,576]{3,4,2,1,0:T(8,128)(2,1)}, u32[]{:S(2)}) copy-start(bf16[2,1,2,128,576]{3,4,2,1,0:T(8,128)(2,1)} %param.14) | copy-start | bytes 1769476
  0.6 13.6 %copy-start.2 = (bf16[2,1,2,576]{3,2,1,0:T(2,128)(2,1)S(1)}, bf16[2,1,2,576]{3,2,1,0:T(2,128)(2,1)}, u32[]{:S(2)}) copy-start(bf16[2,1,2,576]{3,2,1,0:T(2,128)(2,1)} %param.15) | copy-start | bytes 13828
  2.4 22.2 %all-to-all-start = ((bf16[16,4,3584]{2,1,0:T(4,128)(2,1)}), bf16[16,4,3584]{2,1,0:T(4,128)(2,1)S(1)}, u32[]{:S(2)}, u32[]{:S(2)}) async-start(bf16[16,4,3584]{2,1,0:T(4,128)(2,1)} %broadcast_in_dim.28), calls=%async_computation | async-start | bytes 917504 | tf_op jit(solution)/shard_map/all_to_all | solution.py:116
  24.7 1.9 %collective-permute-start.3 = (bf16[64,3584]{1,0:T(8,128)(2,1)S(1)}, bf16[64,3584]{1,0:T(8,128)(2,1)S(1)}, u32[]{:S(2)}, u32[]{:S(2)}) collective-permute-start(bf16[64,3584]{1,0:T(8,128)(2,1)S(1)} %reshape.104), channel_id=1, source_target_pairs={{0,16},{16,0},{1,17},{17,1},{2,18},{18,2},{3,19},{19,3},{4,20},{20... | collective-permute-start | bytes 1376264 | tf_op jit(solution)/shard_map/ppermute | solution.py:112
  29.3 4.7 %copy-start.4 = (s32[16,2]{0,1:T(2,128)S(1)}, s32[16,2]{0,1:T(2,128)}, u32[]{:S(2)}) copy-start(s32[16,2]{0,1:T(2,128)} %param.12) | copy-start | bytes 388
  29.3 4.7 %copy-start.5 = (s32[16,2]{0,1:T(2,128)S(1)}, s32[16,2]{0,1:T(2,128)}, u32[]{:S(2)}) copy-start(s32[16,2]{0,1:T(2,128)} %param.13) | copy-start | bytes 388
  33.8 19.8 %copy-start.6 = (bf16[2,1,2,8]{3,2,1,0:T(2,128)(2,1)S(1)}, bf16[2,1,2,8]{3,2,1,0:T(2,128)(2,1)}, u32[]{:S(2)}) copy-start(bf16[2,1,2,8]{3,2,1,0:T(2,128)(2,1)} %param.18) | copy-start | bytes 196
  33.8 20.0 %copy-start.3 = (s32[2,1,2,8]{3,2,1,0:T(2,128)S(1)}, s32[2,1,2,8]{3,2,1,0:T(2,128)}, u32[]{:S(2)}) copy-start(s32[2,1,2,8]{3,2,1,0:T(2,128)} %param.17) | copy-start | bytes 388
  33.9 11.8 %collective-permute-start.4 = (bf16[64,3584]{1,0:T(8,128)(2,1)S(1)}, bf16[64,3584]{1,0:T(8,128)(2,1)S(1)}, u32[]{:S(2)}, u32[]{:S(2)}) collective-permute-start(bf16[64,3584]{1,0:T(8,128)(2,1)S(1)} %slice.35), channel_id=1, source_target_pairs={{0,16},{16,0},{1,17},{17,1},{2,18},{18,2},{3,19},{19,3},{4,20},{20... | collective-permute-start | bytes 1376264 | tf_op jit(solution)/shard_map/ppermute | solution.py:112
  39.0 27.7 %copy-start = (bf16[2,2,128,512]{3,2,1,0:T(8,128)(2,1)S(1)}, bf16[2,2,128,512]{3,2,1,0:T(8,128)(2,1)}, u32[]{:S(2)}) copy-start(bf16[2,2,128,512]{3,2,1,0:T(8,128)(2,1)} %attend.1) | copy-start | bytes 1572868
  40.1 13.9 %collective-permute-start.1 = (bf16[1,2,128,512]{3,2,1,0:T(8,128)(2,1)S(1)}, bf16[1,2,128,512]{3,2,1,0:T(8,128)(2,1)S(1)}, u32[]{:S(2)}, u32[]{:S(2)}) collective-permute-start(bf16[1,2,128,512]{3,2,1,0:T(8,128)(2,1)S(1)} %get-tuple-element.11), channel_id=1, source_target_pairs={{0,15},{1,0},{2,1},{3,2},{4,3},{5,4},{6,5},{7,6},{8,7},{9,8},{10,9... | collective-permute-start | bytes 786440 | tf_op jit(solution)/shard_map/ppermute | solution.py:79
  42.6 12.9 %collective-permute-start.2 = (bf16[1,2,128,512]{3,2,1,0:T(8,128)(2,1)S(1)}, bf16[1,2,128,512]{3,2,1,0:T(8,128)(2,1)S(1)}, u32[]{:S(2)}, u32[]{:S(2)}) collective-permute-start(bf16[1,2,128,512]{3,2,1,0:T(8,128)(2,1)S(1)} %get-tuple-element.11), channel_id=1, source_target_pairs={{0,1},{1,2},{2,3},{3,4},{4,5},{5,6},{6,7},{7,8},{8,9},{9,10},{10,1... | collective-permute-start | bytes 786440 | tf_op jit(solution)/shard_map/ppermute | solution.py:78
  42.6 24.1 %collective-permute-start = (bf16[1,2,128,512]{3,2,1,0:T(8,128)(2,1)S(1)}, bf16[1,2,128,512]{3,2,1,0:T(8,128)(2,1)}, u32[]{:S(2)}, u32[]{:S(2)}) collective-permute-start(bf16[1,2,128,512]{3,2,1,0:T(8,128)(2,1)S(1)} %get-tuple-element.10), channel_id=1, source_target_pairs={{0,8},{1,9},{2,10},{3,11},{4,12},{5,13},{6,14},{7,15},{8,0},{9,1},... | collective-permute-start | bytes 786440 | tf_op jit(solution)/shard_map/ppermute | solution.py:77
  46.6 26.8 %all-to-all-start.1 = ((bf16[16,4,3584]{2,1,0:T(4,128)(2,1)}), bf16[16,4,3584]{2,1,0:T(4,128)(2,1)S(1)}, u32[]{:S(2)}, u32[]{:S(2)}) async-start(bf16[16,4,3584]{2,1,0:T(4,128)(2,1)} %reshape.105), calls=%async_computation.1 | async-start | bytes 917504 | tf_op jit(solution)/shard_map/all_to_all | solution.py:134

commit v2 on v1

--- a/solution.py
+++ b/solution.py
@@ -4,6 +4,7 @@
 from jax.experimental import pallas as pl
 from jax.experimental.pallas import tpu as pltpu
 from jax.sharding import PartitionSpec as P
+
 
 KV_RANK = 512
 HEAD_QK = 192
@@ -67,16 +68,20 @@
     )(own_lengths, queries, cache, fresh)
 
 
-def relocate(computed, new_home, ranks, own_rank):
-    requests = computed.shape[0]
+def travel(even, odd, ranks):
     half = ranks // 2
     across = [(e, (e + half) % ranks) for e in range(ranks)]
     ahead = [(e, (e + 1) % ranks) for e in range(ranks)]
     behind = [(e, (e - 1) % ranks) for e in range(ranks)]
-    even, odd = computed[0::2], computed[1::2]
     far = lax.ppermute(even, "ep", across)
     left = lax.ppermute(odd, "ep", ahead)
     right = lax.ppermute(odd, "ep", behind)
+    return far, left, right
+
+
+def relocate(computed, arrived, new_home, ranks, own_rank):
+    requests = computed.shape[0]
+    far, left, right = arrived
     anchor = new_home[own_rank]
     results = []
     for request in range(requests):
@@ -119,22 +124,28 @@
     computed = attend(
         lengths[own_rank], queries, latent_cache, jnp.swapaxes(new_latent[:, 0], 0, 1)
     )
-    attended = relocate(computed, new_home, ranks, own_rank)
+    mine, computed, even, odd = lax.optimization_barrier(
+        (mine, computed, computed[0::2], computed[1::2])
+    )
+    arrived = travel(even, odd, ranks)
 
     tokens = jnp.concatenate([mine] + [shift(mine, step) for step in range(1, slices)], 0)
     gate_part = jnp.dot(tokens, w_gate[0], preferred_element_type=jnp.float32)
     up_part = jnp.dot(tokens, w_up[0], preferred_element_type=jnp.float32)
     units = (jax.nn.silu(gate_part) * up_part).astype(jnp.bfloat16)
-    slice_out = jnp.dot(units, w_down[0], preferred_element_type=jnp.float32).astype(jnp.bfloat16)
+    slice_out = jnp.dot(units, w_down[0], preferred_element_type=jnp.float32)
+    slice_out = slice_out.astype(jnp.bfloat16)
     parts = slice_out.reshape(slices, ranks * own_rows, width)
     whole = parts[0].astype(jnp.float32)
     for step in range(1, slices):
         whole = whole + shift(parts[step], -step).astype(jnp.float32)
     whole = whole.astype(jnp.bfloat16)
+    whole, arrived = lax.optimization_barrier((whole, arrived))
     returned = lax.all_to_all(
         whole.reshape(ranks, own_rows, width), "ep", split_axis=0, concat_axis=0, tiled=True
     )
 
+    attended = relocate(computed, arrived, new_home, ranks, own_rank)
     sigmoid_part = jax.nn.sigmoid(route_logits[:, 0].astype(jnp.float32))
     gates = 2.5 * sigmoid_part / jnp.sum(sigmoid_part, -1, keepdims=True)
     rank_ids = jnp.arange(ranks, dtype=jnp.int32)

time: 74.8 us -> 79.2 us (1.059)
  waiting for transfers between devices: 29.9 us -> 33.5 us
    all_to_all x1, waiting for transfers between devices: 9.73 us -> 3.67 us  [shards(): mine = lax.all_to_all(copies, 'ep', split_axis=0, concat_axis=0, tiled=True)]
    all_to_all x1, waiting for transfers between devices: 5.7 us -> 11.7 us  [shards(): lax.all_to_all(whole.reshape(ranks, own_rows, width), 'ep', split_axis=0,...]
    ppermute x3, waiting for transfers between devices: 12.7 us -> 16.3 us  [the longest x1 7.57 us: travel(): far = lax.ppermute(even, 'ep', across)]
    ppermute x3, starting transfers between devices: 3 us -> 5.68 us  [the longest x1 5.04 us: travel(): right = lax.ppermute(odd, 'ep', behind)]
    all_to_all x1, starting transfers between devices: 6.99 us -> 4.95 us  [shards(): lax.all_to_all(whole.reshape(ranks, own_rows, width), 'ep', split_axis=0,...]
  transfers between devices with their start and end apart: 7 -> 7, of which waited for: 5 -> 6; matrix products, arithmetic and copies ran while one was open for 12% -> 10% of each run, Pallas kernels for 6% -> 5%
where the time goes in v2:
time: 79.2 us; the launch traced here: 78.7 us
  waiting for transfers between devices  33.5 us (42%)
  starting transfers between devices  19.2 us (24%)
  local copies, waits for them, and re-layouts  10.9 us (14%)
  matrix products  7.13 us (9%)
  Pallas kernels  4.27 us (5%)
  between operations  2.84 us (4%)
  other arithmetic  0.82 us (1%)
    all_to_all x1, waiting for transfers between devices, shards(): lax.all_to_all(whole.reshape(ranks, own_rows, width), 'ep', split_axis=0,...  11.7 us
    all_to_all x1, starting transfers between devices, shards(): mine = lax.all_to_all(copies, 'ep', split_axis=0, concat_axis=0, tiled=True)  8.34 us
    ppermute x1, waiting for transfers between devices, travel(): far = lax.ppermute(even, 'ep', across)  7.57 us
    ppermute x1, waiting for transfers between devices, travel(): left = lax.ppermute(odd, 'ep', ahead)  7.14 us
    ppermute x1, starting transfers between devices, travel(): right = lax.ppermute(odd, 'ep', behind)  5.04 us
    unnamed x19, local copies, waits for them, and re-layouts  5.04 us
    all_to_all x1, starting transfers between devices, shards(): lax.all_to_all(whole.reshape(ranks, own_rows, width), 'ep', split_axis=0,...  4.95 us
    dot_general x1, matrix products, shards(): slice_out = jnp.dot(units, w_down[0], preferred_element_type=jnp.float32)  4.45 us
  transfers between devices with their start and end apart: 7, of which 6 were waited for; matrix products, arithmetic and copies ran while one was open for 10% of the time, Pallas kernels for 5%

profile of v2, /device:TPU:0, one launch (start us, length us, event | category | flops | bytes accessed | tf_op | source)
XLA Modules:
  0.0 78.7 jit_solution(411373577672247236)
XLA Ops:
  0.7 0.8 %broadcast_in_dim.26 = bf16[4,3584]{1,0:T(4,128)(2,1)S(1)} reshape(bf16[2,1,2,3584]{3,2,1,0:T(2,128)(2,1)} %param.16) | data formatting | bytes 57344 | tf_op jit(solution)/shard_map/broadcast_in_dim | solution.py:120
  1.5 0.9 %broadcast_in_dim.27 = bf16[16,4,3584]{2,1,0:T(4,128)(2,1)} broadcast(bf16[4,3584]{1,0:T(4,128)(2,1)S(1)} %broadcast_in_dim.26), dimensions={1,2} | broadcast | bytes 487424 | tf_op jit(solution)/shard_map/broadcast_in_dim | solution.py:120
  2.4 8.3 %all-to-all-start = ((bf16[16,4,3584]{2,1,0:T(4,128)(2,1)}), bf16[16,4,3584]{2,1,0:T(4,128)(2,1)S(1)}, u32[]{:S(2)}, u32[]{:S(2)}) async-start(bf16[16,4,3584]{2,1,0:T(4,128)(2,1)} %broadcast_in_dim.27), calls=%async_computation | async-start | bytes 917504 | tf_op jit(solution)/shard_map/all_to_all | solution.py:121
  10.7 2.4 %copy.20.cache_ref = bf16[1,2,512,576]{3,2,1,0:T(8,128)(2,1)} copy(bf16[1,2,512,576]{2,3,1,0:T(8,128)(2,1)} %param.11) | data formatting | bytes 2359296 | tf_op args[0]
  13.1 1.1 %copy.19.query_ref = bf16[2,1,2,128,576]{4,3,2,1,0:T(8,128)(2,1)} copy(bf16[2,1,2,128,576]{3,4,2,1,0:T(8,128)(2,1)S(1)} %copy-done.2) | data formatting | bytes 1179648 | tf_op args[3]
  14.3 0.6 copy.24
  14.9 0.7 dynamic-slice_reduce_fusion.length_ref
  15.6 4.3 %attend.1 = bf16[2,2,128,512]{3,2,1,0:T(8,128)(2,1)} custom-call(s32[2]{0:T(128)} %dynamic-slice_reduce_fusion.length_ref, bf16[2,1,2,128,576]{4,3,2,1,0:T(8,128)(2,1)} %copy.19.query_ref, bf16[1,2,512,576]{3,2,1,0:T(8,128)(2,1)} %copy.20.cache_ref, bf16[2,2,576]{2,1,0:T(2,128)(2,1)} %bitcast.34), custom_call_target="tpu_custom_call" | custom-call | tf_op jit(solution)/shard_map/attend/pallas_call | solution.py:54
  19.8 1.1 %fusion.12 = (bf16[1,2,128,512]{3,2,1,0:T(8,128)(2,1)S(1)}, bf16[1,2,128,512]{3,2,1,0:T(8,128)(2,1)S(1)}) fusion(bf16[2,2,128,512]{3,2,1,0:T(8,128)(2,1)} %attend.1), kind=kLoop, calls=%fused_computation.24 | loop fusion | bytes 1048576 | tf_op jit(solution)/shard_map/slice | solution.py:128
  20.9 3.7 %all-to-all-done = bf16[16,4,3584]{2,1,0:T(4,128)(2,1)S(1)} async-done(((bf16[16,4,3584]{2,1,0:T(4,128)(2,1)}), bf16[16,4,3584]{2,1,0:T(4,128)(2,1)S(1)}, u32[]{:S(2)}, u32[]{:S(2)}) %all-to-all-start) | async-done | bytes 458784 | tf_op jit(solution)/shard_map/all_to_all | solution.py:121
  24.6 0.1 reshape.104
  24.8 1.8 %collective-permute-done = bf16[64,3584]{1,0:T(8,128)(2,1)S(1)} collective-permute-done((bf16[64,3584]{1,0:T(8,128)(2,1)S(1)}, bf16[64,3584]{1,0:T(8,128)(2,1)S(1)}, u32[]{:S(2)}, u32[]{:S(2)}) %collective-permute-start) | collective-permute-done | bytes 458784 | tf_op jit(solution)/shard_map/ppermute | solution.py:117
  26.6 2.7 %fusion.1 = f32[128,512]{1,0:T(8,128)S(1)} fusion(bf16[128,3584]{1,0:T(8,128)(2,1)S(1)} %constant_dynamic-update-slice_fusion, bf16[1,3584,512]{2,1,0:T(8,128)(2,1)} %param.20), kind=kOutput, calls=%fused_computation.2 | convolution fusion | flops 469762048 | bytes 4849664 | tf_op jit(solution)/shard_map/dot_general | solution.py:134
  29.3 4.5 %convolution_convert_fusion = bf16[128,3584]{1,0:T(8,128)(2,1)S(1)} fusion(bf16[1,512,3584]{2,1,0:T(8,128)(2,1)} %param.21, f32[128,512]{1,0:T(8,128)S(1)} %fusion.1, bf16[128,3584]{1,0:T(8,128)(2,1)S(1)} %constant_dynamic-update-slice_fusion, bf16[1,3584,512]{2,1,0:T(8,128)(2,1)} %param.19), kind=kOutput, calls=%fused_computation | convolution fusion | flops 940376064 | bytes 9437184 | tf_op jit(solution)/shard_map/dot_general | solution.py:136
  33.8 0.2 collective-permute-start.1
  34.1 0.6 fusion.13
  36.7 0.6 collective-permute-start.3
  37.4 5.0 %collective-permute-start.4 = (bf16[1,2,128,512]{3,2,1,0:T(8,128)(2,1)S(1)}, bf16[1,2,128,512]{3,2,1,0:T(8,128)(2,1)S(1)}, u32[]{:S(2)}, u32[]{:S(2)}) collective-permute-start(bf16[1,2,128,512]{3,2,1,0:T(8,128)(2,1)S(1)} %get-tuple-element.13), channel_id=1, source_target_pairs={{0,15},{1,0},{2,1},{3,2},{4,3},{5,4},{6,5},{7,6},{8,7},{9,8},{10,9... | collective-permute-start | bytes 786440 | tf_op jit(solution)/shard_map/ppermute | solution.py:78
  42.4 0.1 add_convert_fusion
  42.5 7.1 %collective-permute-done.3 = bf16[1,2,128,512]{3,2,1,0:T(8,128)(2,1)S(1)} collective-permute-done((bf16[1,2,128,512]{3,2,1,0:T(8,128)(2,1)S(1)}, bf16[1,2,128,512]{3,2,1,0:T(8,128)(2,1)S(1)}, u32[]{:S(2)}, u32[]{:S(2)}) %collective-permute-start.3) | collective-permute-done | bytes 262176 | tf_op jit(solution)/shard_map/ppermute | solution.py:77
  49.7 1.6 %collective-permute-done.4 = bf16[1,2,128,512]{3,2,1,0:T(8,128)(2,1)S(1)} collective-permute-done((bf16[1,2,128,512]{3,2,1,0:T(8,128)(2,1)S(1)}, bf16[1,2,128,512]{3,2,1,0:T(8,128)(2,1)S(1)}, u32[]{:S(2)}, u32[]{:S(2)}) %collective-permute-start.4) | collective-permute-done | bytes 262176 | tf_op jit(solution)/shard_map/ppermute | solution.py:78
  51.3 7.6 %collective-permute-done.2 = bf16[1,2,128,512]{3,2,1,0:T(8,128)(2,1)} collective-permute-done((bf16[1,2,128,512]{3,2,1,0:T(8,128)(2,1)S(1)}, bf16[1,2,128,512]{3,2,1,0:T(8,128)(2,1)}, u32[]{:S(2)}, u32[]{:S(2)}) %collective-permute-start.2) | collective-permute-done | bytes 262176 | tf_op jit(solution)/shard_map/ppermute | solution.py:76
  58.9 0.9 %reshape.105 = bf16[16,4,3584]{2,1,0:T(4,128)(2,1)} reshape(bf16[64,3584]{1,0:T(8,128)(2,1)S(1)} %add_convert_fusion) | data formatting | bytes 917504 | tf_op jit(solution)/shard_map/reshape | solution.py:145
  59.8 5.0 %all-to-all-start.1 = ((bf16[16,4,3584]{2,1,0:T(4,128)(2,1)}), bf16[16,4,3584]{2,1,0:T(4,128)(2,1)S(1)}, u32[]{:S(2)}, u32[]{:S(2)}) async-start(bf16[16,4,3584]{2,1,0:T(4,128)(2,1)} %reshape.105), calls=%async_computation.1 | async-start | bytes 917504 | tf_op jit(solution)/shard_map/all_to_all | solution.py:144
  64.7 0.1 fusion.11
  64.9 0.1 select_reduce_fusion
  65.0 0.1 copy.21
  65.1 0.1 select_bitcast_fusion.1
  65.2 0.8 %copy.22 = bf16[2,1,2,128,512]{4,3,2,1,0:T(8,128)(2,1)} copy(bf16[2,1,2,128,512]{4,3,0,2,1:T(8,128)(2,1)S(1)} %maximum_bitcast_fusion) | data formatting | bytes 1048576
  66.1 11.7 %all-to-all-done.1 = bf16[16,4,3584]{2,1,0:T(4,128)(2,1)S(1)} async-done(((bf16[16,4,3584]{2,1,0:T(4,128)(2,1)}), bf16[16,4,3584]{2,1,0:T(4,128)(2,1)S(1)}, u32[]{:S(2)}, u32[]{:S(2)}) %all-to-all-start.1) | async-done | bytes 458784 | tf_op jit(solution)/shard_map/all_to_all | solution.py:144
  77.8 0.3 multiply_reduce_fusion
  78.1 0.6 convert_element_type.47
  (23 shorter events, 0.4 us)
Async XLA Ops:
  0.6 14.2 %copy-start = (s32[16,2]{0,1:T(2,128)S(1)}, s32[16,2]{0,1:T(2,128)}, u32[]{:S(2)}) copy-start(s32[16,2]{0,1:T(2,128)} %param.12) | copy-start | bytes 388
  0.6 12.5 %copy-start.2 = (bf16[2,1,2,128,576]{3,4,2,1,0:T(8,128)(2,1)S(1)}, bf16[2,1,2,128,576]{3,4,2,1,0:T(8,128)(2,1)}, u32[]{:S(2)}) copy-start(bf16[2,1,2,128,576]{3,4,2,1,0:T(8,128)(2,1)} %param.14) | copy-start | bytes 1769476
  0.7 13.6 %copy-start.3 = (bf16[2,1,2,576]{3,2,1,0:T(2,128)(2,1)S(1)}, bf16[2,1,2,576]{3,2,1,0:T(2,128)(2,1)}, u32[]{:S(2)}) copy-start(bf16[2,1,2,576]{3,2,1,0:T(2,128)(2,1)} %param.15) | copy-start | bytes 13828
  2.4 22.2 %all-to-all-start = ((bf16[16,4,3584]{2,1,0:T(4,128)(2,1)}), bf16[16,4,3584]{2,1,0:T(4,128)(2,1)S(1)}, u32[]{:S(2)}, u32[]{:S(2)}) async-start(bf16[16,4,3584]{2,1,0:T(4,128)(2,1)} %broadcast_in_dim.27), calls=%async_computation | async-start | bytes 917504 | tf_op jit(solution)/shard_map/all_to_all | solution.py:121
  24.7 1.9 %collective-permute-start = (bf16[64,3584]{1,0:T(8,128)(2,1)S(1)}, bf16[64,3584]{1,0:T(8,128)(2,1)S(1)}, u32[]{:S(2)}, u32[]{:S(2)}) collective-permute-start(bf16[64,3584]{1,0:T(8,128)(2,1)S(1)} %reshape.104), channel_id=1, source_target_pairs={{0,16},{16,0},{1,17},{17,1},{2,18},{18,2},{3,19},{19,3},{4,20},{20... | collective-permute-start | bytes 1376264 | tf_op jit(solution)/shard_map/ppermute | solution.py:117
  29.3 4.7 %copy-start.5 = (s32[16,2]{0,1:T(2,128)S(1)}, s32[16,2]{0,1:T(2,128)}, u32[]{:S(2)}) copy-start(s32[16,2]{0,1:T(2,128)} %param.13) | copy-start | bytes 388
  33.8 30.9 %copy-start.6 = (bf16[2,1,2,8]{3,2,1,0:T(2,128)(2,1)S(1)}, bf16[2,1,2,8]{3,2,1,0:T(2,128)(2,1)}, u32[]{:S(2)}) copy-start(bf16[2,1,2,8]{3,2,1,0:T(2,128)(2,1)} %param.18) | copy-start | bytes 196
  33.8 31.1 %copy-start.4 = (s32[2,1,2,8]{3,2,1,0:T(2,128)S(1)}, s32[2,1,2,8]{3,2,1,0:T(2,128)}, u32[]{:S(2)}) copy-start(s32[2,1,2,8]{3,2,1,0:T(2,128)} %param.17) | copy-start | bytes 388
  33.8 31.3 %copy-start.1 = (bf16[2,2,128,512]{3,2,1,0:T(8,128)(2,1)S(1)}, bf16[2,2,128,512]{3,2,1,0:T(8,128)(2,1)}, u32[]{:S(2)}) copy-start(bf16[2,2,128,512]{3,2,1,0:T(8,128)(2,1)} %attend.1) | copy-start | bytes 1572868
  33.8 8.6 %collective-permute-start.1 = (bf16[64,3584]{1,0:T(8,128)(2,1)S(1)}, bf16[64,3584]{1,0:T(8,128)(2,1)S(1)}, u32[]{:S(2)}, u32[]{:S(2)}) collective-permute-start(bf16[64,3584]{1,0:T(8,128)(2,1)S(1)} %slice.41), channel_id=1, source_target_pairs={{0,16},{16,0},{1,17},{17,1},{2,18},{18,2},{3,19},{19,3},{4,20},{20... | collective-permute-start | bytes 1376264 | tf_op jit(solution)/shard_map/ppermute | solution.py:117
  36.7 12.9 %collective-permute-start.3 = (bf16[1,2,128,512]{3,2,1,0:T(8,128)(2,1)S(1)}, bf16[1,2,128,512]{3,2,1,0:T(8,128)(2,1)S(1)}, u32[]{:S(2)}, u32[]{:S(2)}) collective-permute-start(bf16[1,2,128,512]{3,2,1,0:T(8,128)(2,1)S(1)} %get-tuple-element.13), channel_id=1, source_target_pairs={{0,1},{1,2},{2,3},{3,4},{4,5},{5,6},{6,7},{7,8},{8,9},{9,10},{10,1... | collective-permute-start | bytes 786440 | tf_op jit(solution)/shard_map/ppermute | solution.py:77
  37.4 13.9 %collective-permute-start.4 = (bf16[1,2,128,512]{3,2,1,0:T(8,128)(2,1)S(1)}, bf16[1,2,128,512]{3,2,1,0:T(8,128)(2,1)S(1)}, u32[]{:S(2)}, u32[]{:S(2)}) collective-permute-start(bf16[1,2,128,512]{3,2,1,0:T(8,128)(2,1)S(1)} %get-tuple-element.13), channel_id=1, source_target_pairs={{0,15},{1,0},{2,1},{3,2},{4,3},{5,4},{6,5},{7,6},{8,7},{9,8},{10,9... | collective-permute-start | bytes 786440 | tf_op jit(solution)/shard_map/ppermute | solution.py:78
  42.4 16.5 %collective-permute-start.2 = (bf16[1,2,128,512]{3,2,1,0:T(8,128)(2,1)S(1)}, bf16[1,2,128,512]{3,2,1,0:T(8,128)(2,1)}, u32[]{:S(2)}, u32[]{:S(2)}) collective-permute-start(bf16[1,2,128,512]{3,2,1,0:T(8,128)(2,1)S(1)} %get-tuple-element.12), channel_id=1, source_target_pairs={{0,8},{1,9},{2,10},{3,11},{4,12},{5,13},{6,14},{7,15},{8,0},{9,1},... | collective-permute-start | bytes 786440 | tf_op jit(solution)/shard_map/ppermute | solution.py:76
  59.8 18.0 %all-to-all-start.1 = ((bf16[16,4,3584]{2,1,0:T(4,128)(2,1)}), bf16[16,4,3584]{2,1,0:T(4,128)(2,1)S(1)}, u32[]{:S(2)}, u32[]{:S(2)}) async-start(bf16[16,4,3584]{2,1,0:T(4,128)(2,1)} %reshape.105), calls=%async_computation.1 | async-start | bytes 917504 | tf_op jit(solution)/shard_map/all_to_all | solution.py:144
